TPU v7x, 256 devices: a whole 4x4x8 slice. The times are simulated.
256 devices in a mesh: seq: 128 (over z, x, y), tp: 2 (over core).
Axes of the slice: x: 4, y: 4, z: 8, core: 2. Of those that a mesh axis runs over, the one named last changes fastest.
Arguments:
- latent: bfloat16 [128, 8, 32, 128], P(None, 'tp', None, 'seq'), may hold values from -8 to 8
- conv_weight: bfloat16 [3, 3, 3, 32, 128], replicated, may hold values from -0.21875 to 0.21875
- conv_bias: float32 [128], replicated, may hold values from -4 to 4
- proj_weight: bfloat16 [128, 32], replicated, may hold values from -0.5 to 0.5
- embed_weight: bfloat16 [32, 2240], replicated, may hold values from -1 to 1
- embed_bias: float32 [2240], replicated, may hold values from -3 to 3
- qkv_weight: bfloat16 [3, 2240, 1120], P(None, None, 'tp'), may hold values from -0.125 to 0.125
Outputs:
- attended: bfloat16 [131072, 1120], P('seq', 'tp')
All inputs are finite; a program needn't handle non-finite values.
Results may differ from a plain program's by a relative error of at most 0.0034.
Values may be sent and summed in bfloat16 or wider, within the bound.
A program may use at most 128 MiB of HBM per device.

v0:
```python
import jax
import jax.numpy as jnp
from jax import lax
from jax.sharding import PartitionSpec as P

DH = 112
CLIPS = 1


epsilon = 1e-06


def extended_2(x, sides, width):
    for axis, dim in sides:
        devices, length = (lax.axis_size(axis), x.shape[dim])
        up = [(i, (i + 1) % devices) for i in range(devices - 1)]
        down = [(j, i) for i, j in up]
        last = lax.slice_in_dim(x, length - width, length, axis=dim)
        first = lax.slice_in_dim(x, 0, width, axis=dim)
        before = lax.ppermute(last, axis, up)
        after = lax.ppermute(first, axis, down)
        x = jnp.concatenate([before, x, after], axis=dim)
    return x


def carried_in(value, axis, join, neutral):
    count, mine = (lax.axis_size(axis), lax.axis_index(axis))
    pieces = jax.tree.map(lambda part: lax.all_gather(part, axis), value)
    subtotal = jax.tree.map(
        lambda part, zero: jnp.full_like(part, 0) + jnp.asarray(zero, part.dtype), value, neutral
    )

    def lap(position, subtotal):
        longer = join(subtotal, jax.tree.map(lambda part: part[position], pieces))
        return jax.tree.map(lambda new, old: jnp.where(position < mine, new, old), longer, subtotal)

    return lax.fori_loop(0, count - 1, lap, subtotal)


def conv_block(extended, latent, conv_weight, conv_bias, proj_weight, position, per_clip):
    height = extended.shape[0] - 2
    width_dev = extended.shape[1] - 2
    nframes = extended.shape[3] - 2
    pieces = []
    for frame_step in range(3):
        window = extended[:, :, :, frame_step : frame_step + nframes]
        if frame_step == 0:
            window = window * (position >= 1).astype(window.dtype)
        if frame_step == 2:
            window = window * (position <= per_clip - 2).astype(window.dtype)
        for row_step in range(3):
            for col_step in range(3):
                pieces.append(window[row_step : row_step + height, col_step : col_step + width_dev])
    patches = jnp.concatenate(pieces, axis=2)
    kernel = conv_weight.reshape(-1, conv_weight.shape[-1])
    conv = jnp.einsum("rckf,ko->rcof", patches, kernel, preferred_element_type=jnp.float32)
    conv = conv + conv_bias[None, None, :, None]
    act = jax.nn.silu(conv).astype(jnp.bfloat16)
    mixed = jnp.einsum("rcof,oi->rcif", act, proj_weight, preferred_element_type=jnp.float32)
    return (mixed + latent.astype(jnp.float32)).astype(jnp.bfloat16)


def segment_join(earlier, later):
    keep = 1.0 - later[2]
    return (
        later[0] + keep * earlier[0],
        later[1] + keep * earlier[1],
        jnp.maximum(earlier[2], later[2]),
    )


def per_device(latent, conv_weight, conv_bias, proj_weight, embed_weight, embed_bias, qkv_weight):
    devices = lax.axis_size("seq")
    frames_dev = latent.shape[3]
    per_clip = frames_dev * devices // CLIPS
    bands = lax.all_to_all(latent, "seq", split_axis=0, concat_axis=3, tiled=True)
    padded = extended_2(bands, (("seq", 0), ("tp", 1)), 1)
    extended = jnp.pad(padded, ((0, 0), (0, 0), (0, 0), (1, 1)))
    position = jnp.arange(bands.shape[3], dtype=jnp.int32) % per_clip
    band_mixed = conv_block(
        extended, bands, conv_weight, conv_bias, proj_weight, position, per_clip
    )
    blocks = lax.all_to_all(band_mixed, "seq", split_axis=3, concat_axis=0, tiled=True)
    gathered = lax.all_gather(blocks, "tp", axis=1, tiled=True)
    frame_count = gathered.shape[3]
    embedded = jnp.einsum(
        "hwcf,cd->fhwd", gathered, embed_weight, preferred_element_type=jnp.float32
    )
    embedded = (embedded + embed_bias).astype(jnp.bfloat16).reshape(-1, embed_weight.shape[1])
    projected = jnp.einsum("td,sde->ste", embedded, qkv_weight, preferred_element_type=jnp.float32)
    projected = projected.astype(jnp.bfloat16)
    heads_dev = qkv_weight.shape[2] // DH
    queries = jax.nn.relu(projected[0]).reshape(frame_count, -1, heads_dev, DH)
    keys = jax.nn.relu(projected[1]).reshape(frame_count, -1, heads_dev, DH)
    values = projected[2].reshape(frame_count, -1, heads_dev, DH)
    frame_states = jnp.einsum("fthi,fthj->fhij", keys, values, preferred_element_type=jnp.float32)
    frame_norms = jnp.sum(keys.astype(jnp.float32), axis=1)
    own_state = jnp.sum(frame_states, axis=0)
    own_norm = jnp.sum(frame_norms, axis=0)
    half_span = devices // CLIPS
    clip_start = (lax.axis_index("seq") % half_span == 0).astype(jnp.float32)
    identity = (jnp.zeros_like(own_state), jnp.zeros_like(own_norm), jnp.zeros((), jnp.float32))
    prev_state, prev_norm, flagged = carried_in(
        (own_state, own_norm, clip_start), "seq", segment_join, identity
    )
    prev_state = prev_state * (1.0 - clip_start)
    prev_norm = prev_norm * (1.0 - clip_start)
    running_state = prev_state[None] + jnp.cumsum(frame_states, axis=0)
    running_norm = prev_norm[None] + jnp.cumsum(frame_norms, axis=0)
    query_wide = queries.astype(jnp.float32)
    numer = jnp.einsum(
        "fthi,fhij->fthj", query_wide, running_state, precision=lax.Precision.HIGHEST
    )
    denom = (
        jnp.einsum("fthi,fhi->fth", query_wide, running_norm, precision=lax.Precision.HIGHEST)
        + epsilon
    )
    result = (numer / denom[..., None]).astype(jnp.bfloat16)
    return result.reshape(-1, heads_dev * DH)


def solution(mesh):
    return jax.shard_map(
        per_device,
        mesh=mesh,
        in_specs=(P(None, "tp", None, "seq"), P(), P(), P(), P(), P(), P(None, None, "tp")),
        out_specs=P("seq", "tp"),
        check_vma=False,
    )
```

profile of v0, /device:TPU:8, one launch (start us, length us, event | category | flops | bytes accessed | tf_op | source)
XLA Modules:
  0.0 1104.3 jit_solution(18030080865647262515)
XLA Ops:
  7.5 27.0 %all_to_all.36 = bf16[128,4,32,1]{2,1,3,0:T(4,128)(2,1)S(1)} all-to-all(bf16[128,4,32,1]{2,1,3,0:T(4,128)(2,1)S(1)} %copy.16), channel_id=1, replica_groups=mesh['seq'=128,'tp'=2] {'seq'}, dimensions={0} | all-to-all | bytes 65536 | tf_op jit(solution)/shard_map/all_to_all | solution.py:76
  34.6 3.4 collective-permute-start.1
  37.9 2.5 collective-permute-start
  40.4 3.3 collective-permute-done
  43.7 1.3 collective-permute-start.2
  45.0 1.3 collective-permute-start.3
  46.4 1.8 collective-permute-done.3
  49.9 24.4 %all_to_all.37 = bf16[1,4,32,128]{2,1,0,3:T(4,128)(2,1)S(1)} all-to-all(bf16[1,4,32,128]{2,1,0,3:T(4,128)(2,1)S(1)} %copy.19), channel_id=1, replica_groups=mesh['seq'=128,'tp'=2] {'seq'}, dimensions={3} | all-to-all | bytes 65536 | tf_op jit(solution)/shard_map/all_to_all | solution.py:83
  74.4 1.9 all-gather
  76.3 3.6 fusion.3
  80.0 7.0 copy.21
  87.0 11.9 %convert_bitcast_fusion = bf16[3,1024,560]{1,2,0:T(8,128)(2,1)S(1)} fusion(bf16[3,2240,560]{1,2,0:T(8,128)(2,1)} %param.15, bf16[1,128,8,2240]{3,2,1,0:T(8,128)(2,1)} %copy.21), kind=kOutput, calls=%fused_computation.9 | convolution fusion | flops 7708753920 | bytes 15554560 | tf_op jit(solution)/shard_map/td,sde->ste/dot_general | solution.py:90
  99.1 1.5 copy-done.1
  100.6 1.2 fusion.40
  103.2 349.0 %all-reduce.1 = f32[128]{0:T(128)S(1)} all-reduce(f32[128]{0:T(128)S(1)} %dynamic-update-slice), channel_id=1, replica_groups=mesh['seq'=128,'tp'=2] {'seq'}, use_global_device_ids=true, to_apply=%add.1 | all-reduce | flops 128 | bytes 1024
  452.2 1.6 convert_reduce_fusion
  453.9 340.9 %all_gather.21 = f32[128,5,112]{2,1,0:T(8,128)S(1)} all-gather(f32[1,5,112]{2,1,0:T(8,128)S(1)} %reduce_sum.16), channel_id=1, replica_groups=mesh['seq'=128,'tp'=2] {'seq'}, dimensions={0}, use_global_device_ids=true | all-gather | bytes 288960 | tf_op jit(solution)/shard_map/all_gather | solution.py:28
  794.8 299.6 %while.16 = (s32[]{:T(128)}, f32[5,112,112]{2,1,0:T(8,128)S(1)}, f32[5,112]{1,0:T(8,128)S(1)}, s32[]{:T(128)}, f32[128,5,112,112]{3,2,1,0:T(8,128)}, /*index=5*/...) while((s32[]{:T(128)}, f32[5,112,112]{2,1,0:T(8,128)S(1)}, ...), condition=%wide.region_2.3_spmd.clone, body=%wide.region_1.2_spmd.clone.sunk | while | flops 253125 | bytes 759531 | solution.py:37
  796.0 1.2 fusion.49
  798.3 1.2 fusion.49
  803.1 1.2 fusion.49
  805.4 1.2 fusion.49
  810.1 1.2 fusion.49
  1095.4 2.1 fusion.8
  (443 shorter events, 222.1 us)
Async XLA Ops:
  6.5 42.3 %copy-start = (bf16[3,3,3,32,128]{4,3,2,1,0:T(8,128)(2,1)S(1)}, bf16[3,3,3,32,128]{4,3,2,1,0:T(8,128)(2,1)}, u32[]{:S(2)}) copy-start(bf16[3,3,3,32,128]{4,3,2,1,0:T(8,128)(2,1)} %param.10) | copy-start | bytes 663556
  6.5 788.3 %all-gather.4.cloned.1.call-start = ((), (), s32[]{:S(2)}) async-start(), calls=%async_computation.2 | async-start | bytes 36986880 | tf_op jit(solution)/shard_map/all_gather | solution.py:28
  34.6 5.9 collective-permute-start.1
  37.9 5.8 collective-permute-start
  43.7 2.6 collective-permute-start.2
  45.0 3.1 collective-permute-start.3
  48.4 0.7 copy-start.5
  48.4 0.7 copy-start.6
  49.1 27.2 %copy-start.3 = (bf16[32,2240]{1,0:T(8,128)(2,1)S(1)}, bf16[32,2240]{1,0:T(8,128)(2,1)}, u32[]{:S(2)}) copy-start(bf16[32,2240]{1,0:T(8,128)(2,1)} %param.13) | copy-start | bytes 430084
  49.1 27.2 %copy-start.4 = (f32[2240]{0:T(1024)S(1)}, f32[2240]{0:T(1024)}, u32[]{:S(2)}) copy-start(f32[2240]{0:T(1024)} %param.14) | copy-start | bytes 26884
  98.9 1.7 copy-start.1
  100.6 1.3 copy-start.7
  1094.4 1.0 copy-start.2
Sparse Core Ops, SparseCore 0:
  102.0 213.7 all-gather.3
where the time goes:
time: 1110 us; the launch traced here: 1100 us
  blocking collectives  743 us (67%)
  other arithmetic  154 us (14%)
  local copies, waits for them, and re-layouts  83 us (7%)
  loops' own time  76.8 us (7%)
  matrix products  20.1 us (2%)
  between operations  13.8 us (1%)
    unnamed x1, blocking collectives  349 us
    all_gather x1, blocking collectives, carried_in(): pieces = jax.tree.map(lambda part: lax.all_gather(part, axis), value)  341 us
    select_n x254, other arithmetic, lap(): jnp.where(position < mine, new, old)  152 us
    another operation x1, loops' own time, carried_in(): return lax.fori_loop(0, count - 1, lap, subtotal)  76.8 us
    dynamic_slice x127, local copies, waits for them, and re-layouts, lap(): longer = join(subtotal, jax.tree.map(lambda part: part[position], pieces))  71 us
    all_to_all x1, blocking collectives, per_device(): lax.all_to_all(latent, 'seq', split_axis=0, concat_axis=3, tiled=True)  27 us
    all_to_all x1, blocking collectives, per_device(): lax.all_to_all(band_mixed, 'seq', split_axis=3, concat_axis=0, tiled=True)  24.4 us
  transfers between devices with their start and end apart: 5, of which 2 were waited for; matrix products, arithmetic and copies ran while one was open for 0% of the time, Pallas kernels for 0%

commit v1 on v0

v1 whole, which is shorter than its diff:
```python
import functools

import jax
import jax.numpy as jnp
from jax import lax
from jax.experimental import pallas as pl
from jax.experimental.pallas import tpu as pltpu
from jax.sharding import PartitionSpec as P

MESH = pl.DeviceIdType.MESH
F32 = jnp.float32
BF16 = jnp.bfloat16
DH = 112
HEADS = 5
PLANE = 16
DEPTH = 8
OWNERS = 11
NF = PLANE * DEPTH
TOK = 1024
EPS = 1e-6


def nt(a, b):
    return lax.dot_general(a, b, (((1,), (1,)), ((), ())), preferred_element_type=F32)


def nn(a, b):
    return lax.dot_general(a, b, (((1,), (0,)), ((), ())), preferred_element_type=F32)


def three(value):
    hi = value.astype(BF16).astype(F32)
    rest = value - hi
    mid = rest.astype(BF16).astype(F32)
    return hi, mid, (rest - mid).astype(BF16).astype(F32)


def rows_of(parts, rows, width):
    index = lax.broadcasted_iota(jnp.int32, (rows, width), 0)
    out = jnp.zeros((rows, width), F32)
    for i, part in enumerate(parts):
        out = jnp.where(index == i, jnp.broadcast_to(part, (rows, width)), out)
    return out


def kernel(
    lat, cw, cb, pw, ew, eb, w_hbm, out_hbm,
    frames, w, ea, g, cwt, pat, maug, qaug, perm, kt, qt, sx, r1, rz, tz, p3, px, stage,
    hs, hr, ws, s1, v1, s2, v2, s3, v3, os_,
):
    f = lax.axis_index("seq")
    t = lax.axis_index("tp")
    z, p = f // PLANE, f % PLANE
    o = 1 - t
    nxt, prv = (f + 1) % NF, (f + NF - 1) % NF

    barrier = pltpu.get_barrier_semaphore()

    def greet(seq, core):
        pl.semaphore_signal(barrier, inc=1, device_id=(seq, core), device_id_type=MESH)

    greet(f, o)
    for seq in (nxt, prv):
        greet(seq, t)
        greet(seq, o)

    def greet_plane(k, c):
        greet(z * PLANE + (p + k) % PLANE, t)
        return c

    lax.fori_loop(1, PLANE, greet_plane, 0)

    def greet_depth(k, c):
        greet(((z + k) % DEPTH) * PLANE + p, t)
        return c

    lax.fori_loop(1, DEPTH, greet_depth, 0)

    def wcopy(i):
        return pltpu.make_async_copy(w_hbm.at[i], w.at[i], ws.at[i])

    for i in range(3):
        wcopy(i).start()

    frames[1, t] = lat[...]

    width = ew.shape[1]
    bias = three(eb[...])
    ea[0:32] = ew[...]
    ea[32:64] = ew[...]
    ea[64:80] = rows_of(bias + bias, 16, width).astype(BF16)
    ea[80:128] = jnp.zeros((48, width), BF16)

    wide = jnp.concatenate([cw[...].astype(F32), rows_of(three(cb[...]), 32, 128)], axis=0)
    cwt[...] = wide.T.astype(BF16)
    pat[864:896] = jnp.ones((32, TOK), BF16)

    pl.semaphore_wait(barrier, 5 + PLANE - 1 + DEPTH - 1)

    sends = []
    for i, (slot, seq, core) in enumerate(((0, nxt, t), (2, prv, t), (0, nxt, o), (2, prv, o), (1, f, o))):
        copy = pltpu.make_async_remote_copy(
            src_ref=lat, dst_ref=frames.at[slot, t], send_sem=hs.at[i], recv_sem=hr.at[slot, t],
            device_id=(seq, core), device_id_type=MESH)
        copy.start()
        sends.append(copy)

    lane = lax.broadcasted_iota(jnp.int32, (HEADS * DH, 128), 1)
    low = ((lane >= 32) & (lane < 64)) | (lane >= 67)

    def fold(i, c):
        wcopy(i).wait()
        full = nt(w[i], ea[...])
        hi = full.astype(BF16).astype(F32)
        g[i] = jnp.where(low, full - hi, hi).astype(BF16)
        return c

    lax.fori_loop(0, 3, fold, 0)

    def fill(i, c):
        target = lax.broadcasted_iota(jnp.int32, (128, TOK), 1)
        source = lax.broadcasted_iota(jnp.int32, (128, TOK), 0)
        hit = ((target & 7) == i) & ((target >> 3) == source)
        perm[pl.ds(pl.multiple_of(i * 128, 128), 128)] = jnp.where(hit, 1.0, 0.0).astype(BF16)
        return c

    lax.fori_loop(0, 8, fill, 0)
    sx[...] = jnp.zeros_like(sx)

    def arrived(slot, core, i):
        pltpu.make_async_remote_copy(
            src_ref=lat, dst_ref=frames.at[slot, core], send_sem=hs.at[i], recv_sem=hr.at[slot, core],
            device_id=(f, o), device_id_type=MESH).wait_recv()

    arrived(1, o, 4)
    for slot in (0, 2):
        arrived(slot, t, 0)
        arrived(slot, o, 0)

    row = lax.broadcasted_iota(jnp.int32, (32, TOK), 1) & 127
    none = jnp.zeros((32, 128), BF16)
    here = None
    for a in range(3):
        x = jnp.concatenate([frames[a, c // 4, c % 4] for c in range(8)], axis=1).astype(F32)
        if a == 0:
            x = jnp.where(f > 0, x, 0.0)
        if a == 2:
            x = jnp.where(f < NF - 1, x, 0.0)
        if a == 1:
            here = x
        shifted = (
            jnp.where(row == 0, 0.0, pltpu.roll(x, 1, 1)),
            x,
            jnp.where(row == 127, 0.0, pltpu.roll(x, TOK - 1, 1)),
        )
        for b in range(3):
            y = shifted[b].astype(BF16)
            base = (a * 3 + b) * 96
            pat[base : base + 32] = jnp.concatenate([none, y[:, : TOK - 128]], axis=1)
            pat[base + 32 : base + 64] = y
            pat[base + 64 : base + 96] = jnp.concatenate([y[:, 128:], none], axis=1)
    conv = nn(cwt[...], pat[...])
    act = (conv / (1.0 + jnp.exp(-conv))).astype(BF16)
    mixed = (nn(pw[...], act) + here).astype(BF16)
    maug[0:32] = mixed
    maug[32:64] = mixed
    maug[64:80] = jnp.ones((16, TOK), BF16)
    maug[80:128] = jnp.zeros((48, TOK), BF16)

    kt[...] = jnp.maximum(nn(g[1], maug[...]), 0.0).astype(BF16)
    plus = maug[32:80]
    for h in range(HEADS):
        s = nt(plus, kt[h * DH : (h + 1) * DH])
        sx[2 * h, :, 0:DH] = s[0:16]
        sx[2 * h + 1, :, 0:DH] = s[16:32]
        sx[10, h : h + 1, 0:DH] = s[32:33]

    def one(k, c):
        q = (p + k) % PLANE

        @pl.when(q < OWNERS)
        def _():
            pltpu.make_async_remote_copy(
                src_ref=sx.at[q], dst_ref=r1.at[p], send_sem=s1.at[k], recv_sem=v1.at[p],
                device_id=(z * PLANE + q, t), device_id_type=MESH).start()

        return c

    lax.fori_loop(1, PLANE, one, 0)

    def queries():
        qaug[...] = nn(maug[...], perm[...]).astype(BF16)
        qt[...] = jnp.maximum(nn(g[0], qaug[...]), 0.0).astype(BF16)

    @pl.when(p < OWNERS)
    def _():
        r1[p] = sx[p]

        def got(k, c):
            q = (p + k) % PLANE
            pltpu.make_async_remote_copy(
                src_ref=sx.at[0], dst_ref=r1.at[q], send_sem=s1.at[0], recv_sem=v1.at[q],
                device_id=(f, o), device_id_type=MESH).wait_recv()
            return c

        lax.fori_loop(1, PLANE, got, 0)
        total = r1[0]
        for i in range(1, PLANE):
            total = total + r1[i]
        tz[...] = total

        def two(k, c):
            q = (z + k) % DEPTH
            pltpu.make_async_remote_copy(
                src_ref=tz, dst_ref=rz.at[z], send_sem=s2.at[k], recv_sem=v2.at[z],
                device_id=(q * PLANE + p, t), device_id_type=MESH).start()
            return c

        lax.fori_loop(1, DEPTH, two, 0)
        rz[z] = total

    queries()

    @pl.when(p < OWNERS)
    def _():
        def got(k, c):
            q = (z + k) % DEPTH
            pltpu.make_async_remote_copy(
                src_ref=tz, dst_ref=rz.at[q], send_sem=s2.at[0], recv_sem=v2.at[q],
                device_id=(f, o), device_id_type=MESH).wait_recv()
            return c

        lax.fori_loop(1, DEPTH, got, 0)
        run = jnp.zeros((16, 128), F32)
        for i in range(DEPTH - 1):
            run = run + jnp.where(i < z, rz[i], 0.0)
        for i in range(PLANE):
            p3[i] = run
            run = run + r1[i]

        def three_(k, c):
            q = (p + k) % PLANE
            pltpu.make_async_remote_copy(
                src_ref=p3.at[q], dst_ref=px.at[p], send_sem=s3.at[k], recv_sem=v3.at[p],
                device_id=(z * PLANE + q, t), device_id_type=MESH).start()
            return c

        lax.fori_loop(1, PLANE, three_, 0)
        px[p] = p3[p]

    def back(k, c):
        q = (p + k) % PLANE

        @pl.when(q < OWNERS)
        def _():
            pltpu.make_async_remote_copy(
                src_ref=p3.at[0], dst_ref=px.at[q], send_sem=s3.at[0], recv_sem=v3.at[q],
                device_id=(f, o), device_id_type=MESH).wait_recv()

        return c

    lax.fori_loop(1, PLANE, back, 0)

    norms = px[10] + sx[10]
    for h in range(HEADS):
        s = jnp.concatenate([
            px[2 * h] + sx[2 * h], px[2 * h + 1] + sx[2 * h + 1],
            jnp.broadcast_to(norms[h : h + 1], (16, 128))], axis=0)[:, 0:DH]
        hi = s.astype(BF16)
        lo = (s - hi.astype(F32)).astype(BF16)
        both = nn(jnp.concatenate([hi, lo], axis=0), qt[h * DH : (h + 1) * DH])
        n = both[0:48] + both[48:96]
        den = n[32:33]
        inv = 1.0 / (den + EPS)
        r = n[0:32] * jnp.broadcast_to(inv, (32, TOK))
        ratio = jnp.broadcast_to(den * inv, (16, TOK))
        rows = jnp.concatenate([r, r, ratio], axis=0)
        top = rows.astype(BF16)
        rest = (rows - top.astype(F32)).astype(BF16)
        gv = g[2, h * DH : (h + 1) * DH, 0:80]
        stage[h] = (nn(gv, top) + nn(gv, rest)).astype(BF16)
        pltpu.make_async_copy(stage.at[h], out_hbm.at[h], os_.at[h]).start()

    for copy in sends:
        copy.wait_send()

    def sent(k, c):
        @pl.when((p + k) % PLANE < OWNERS)
        def _():
            pltpu.make_async_remote_copy(
                src_ref=sx.at[0], dst_ref=r1.at[0], send_sem=s1.at[k], recv_sem=v1.at[0],
                device_id=(f, o), device_id_type=MESH).wait_send()

        @pl.when(p < OWNERS)
        def _():
            pltpu.make_async_remote_copy(
                src_ref=p3.at[0], dst_ref=px.at[0], send_sem=s3.at[k], recv_sem=v3.at[0],
                device_id=(f, o), device_id_type=MESH).wait_send()

        return c

    lax.fori_loop(1, PLANE, sent, 0)

    @pl.when(p < OWNERS)
    def _():
        def gone(k, c):
            pltpu.make_async_remote_copy(
                src_ref=tz, dst_ref=rz.at[0], send_sem=s2.at[k], recv_sem=v2.at[0],
                device_id=(f, o), device_id_type=MESH).wait_send()
            return c

        lax.fori_loop(1, DEPTH, gone, 0)

    for h in range(HEADS):
        pltpu.make_async_copy(stage.at[h], out_hbm.at[h], os_.at[h]).wait()


def per_device(latent, conv_weight, conv_bias, proj_weight, embed_weight, embed_bias, qkv_weight):
    width = embed_weight.shape[1]
    lat = jnp.transpose(latent, (1, 3, 2, 0)).reshape(4, 32, 128)
    vmem, anywhere = pl.BlockSpec(memory_space=pltpu.VMEM), pl.BlockSpec(memory_space=pl.ANY)
    dma, vm = pltpu.SemaphoreType.DMA, pltpu.VMEM
    out = pl.pallas_call(
        kernel,
        out_shape=jax.ShapeDtypeStruct((HEADS, DH, TOK), BF16),
        in_specs=[vmem] * 6 + [anywhere],
        out_specs=anywhere,
        scratch_shapes=[
            vm((3, 2, 4, 32, 128), BF16),
            vm((3, HEADS * DH, width), BF16),
            vm((128, width), BF16),
            vm((3, HEADS * DH, 128), BF16),
            vm((128, 896), BF16),
            vm((896, TOK), BF16),
            vm((128, TOK), BF16),
            vm((128, TOK), BF16),
            vm((TOK, TOK), BF16),
            vm((HEADS * DH, TOK), BF16),
            vm((HEADS * DH, TOK), BF16),
            vm((OWNERS, 16, 128), F32),
            vm((PLANE, 16, 128), F32),
            vm((DEPTH, 16, 128), F32),
            vm((16, 128), F32),
            vm((PLANE, 16, 128), F32),
            vm((OWNERS, 16, 128), F32),
            vm((HEADS, DH, TOK), BF16),
            dma((5,)), dma((3, 2)), dma((3,)),
            dma((PLANE,)), dma((PLANE,)), dma((DEPTH,)), dma((DEPTH,)), dma((PLANE,)), dma((PLANE,)),
            dma((HEADS,)),
        ],
        compiler_params=pltpu.CompilerParams(collective_id=0, has_side_effects=True),
    )(
        lat, conv_weight.reshape(864, 128), conv_bias.reshape(1, 128), jnp.transpose(proj_weight),
        embed_weight, embed_bias.reshape(1, width), jnp.transpose(qkv_weight, (0, 2, 1)),
    )
    return jnp.transpose(out.reshape(HEADS * DH, TOK))


def solution(mesh):
    return jax.shard_map(
        per_device,
        mesh=mesh,
        in_specs=(P(None, "tp", None, "seq"), P(), P(), P(), P(), P(), P(None, None, "tp")),
        out_specs=P("seq", "tp"),
        check_vma=False,
    )
```

time: 1110 us -> 38.7 us (0.03)
  the two profiles are of different devices: /device:TPU:8 before, /device:TPU:1 now
where the time goes in v1:
time: 38.7 us; the launch traced here: 38.5 us
  Pallas kernels  34.9 us (90%)
  local copies, waits for them, and re-layouts  3.65 us (9%)
    pallas_call x1, Pallas kernels, per_device(): pl.pallas_call(kernel, out_shape=jax.ShapeDtypeStruct((HEADS, DH, TOK), B...  34.9 us
    unnamed x1, local copies, waits for them, and re-layouts  2.34 us
    reshape x1, local copies, waits for them, and re-layouts, per_device(): embed_bias.reshape(1, width)  1.31 us

profile of v1, /device:TPU:1, one launch (start us, length us, event | category | flops | bytes accessed | tf_op | source)
XLA Modules:
  0.0 38.5 jit_solution(2066186096532425670)
XLA Ops:
  0.0 1.3 %reshape.18.eb = f32[1,2240]{1,0:T(1,128)} reshape(f32[2240]{0:T(1024)} %param.12) | data formatting | bytes 17920 | tf_op jit(solution)/shard_map/reshape | solution.py:354
  1.3 34.9 %shard_map.73 = bf16[5,112,1024]{2,1,0:T(8,128)(2,1)} custom-call(bf16[4,32,128]{2,1,0:T(8,128)(2,1)} %bitcast.15, bf16[864,128]{1,0:T(8,128)(2,1)} %bitcast.14, f32[1,128]{1,0:T(1,128)} %bitcast.17, bf16[32,128]{1,0:T(8,128)(2,1)} %bitcast.16, bf16[32,2240]{1,0:T(8,128)(2,1)} %ew.1, f32[1,2240]{1,0:T(1,128)} %reshape.18.eb, bf16[3,560,2240]{2,1,0:T(8,128)(2,1)} %bitcast.12), custom_call_target="tpu_custom_call" | custom-call | tf_op jit(solution)/shard_map/pallas_call | solution.py:323
  36.2 2.3 %copy.10 = bf16[1024,560]{0,1:T(8,128)(2,1)} copy(bf16[1024,560]{0,1:T(8,128)(2,1)} %bitcast.13) | data formatting | bytes 2293760

commit v2 on v1

v2 whole, which is shorter than its diff:
```python
import functools

import jax
import jax.numpy as jnp
from jax import lax
from jax.experimental import pallas as pl
from jax.experimental.pallas import tpu as pltpu
from jax.sharding import PartitionSpec as P

MESH = pl.DeviceIdType.MESH
F32 = jnp.float32
BF16 = jnp.bfloat16
DH = 112
HEADS = 5
PLANE = 16
DEPTH = 8
OWNERS = 11
NF = PLANE * DEPTH
TOK = 1024
EPS = 1e-6


def nt(a, b):
    return lax.dot_general(a, b, (((1,), (1,)), ((), ())), preferred_element_type=F32)


def nn(a, b):
    return lax.dot_general(a, b, (((1,), (0,)), ((), ())), preferred_element_type=F32)


def three(value):
    hi = value.astype(BF16).astype(F32)
    rest = value - hi
    mid = rest.astype(BF16).astype(F32)
    return hi, mid, (rest - mid).astype(BF16).astype(F32)


def rows_of(parts, rows, width):
    index = lax.broadcasted_iota(jnp.int32, (rows, width), 0)
    out = jnp.zeros((rows, width), F32)
    for i, part in enumerate(parts):
        out = jnp.where(index == i, jnp.broadcast_to(part, (rows, width)), out)
    return out


def kernel(
    lat_hbm, cw_hbm, cb_hbm, pw_hbm, ew_hbm, eb_hbm, w_hbm, total_out, gv_out, qt,
    lat, cw, cb, pw, eb, frames, w, ea, g, cwt, pat, maug, qaug, perm, kt, sx, r1, rz, tz, p3, px,
    ls, hs, hr, ws, s1, v1, s2, v2, s3, v3, tok, ztok,
):
    f = lax.axis_index("seq")
    t = lax.axis_index("tp")
    z, p = f // PLANE, f % PLANE
    o = 1 - t
    x, y = p // 4, p % 4

    def load(src, dst, i):
        return pltpu.make_async_copy(src, dst, ls.at[i])

    loads = [
        load(lat_hbm, lat, 0), load(eb_hbm, eb, 1), load(ew_hbm, ea.at[0:32], 2), load(ew_hbm, ea.at[32:64], 3),
        load(cw_hbm, cw, 4), load(cb_hbm, cb, 5), load(pw_hbm, pw, 6),
    ]
    for copy in loads:
        copy.start()

    def wcopy(i, half):
        rows = pl.ds(half * 288, 288 - 16 * half)
        return pltpu.make_async_copy(w_hbm.at[i, rows], w.at[i, rows], ws.at[i, half])

    for i in (1, 2, 0):
        for half in range(2):
            wcopy(i, half).start()

    barrier = pltpu.get_barrier_semaphore()

    def near(act):
        for ok, seq in ((y > 0, f - 1), (y < 3, f + 1), (x > 0, f - 4), (x < 3, f + 4)):
            pl.when(ok)(functools.partial(act, seq))

    def ahead(step, act, back=True):
        if back:
            pl.when(z >= step)(functools.partial(act, f - step * PLANE))
        if back != "only":
            pl.when(z < DEPTH - step)(functools.partial(act, f + step * PLANE))

    def at_least(value, least, top):
        return (value + top + 1 - least) // (top + 1)

    around = at_least(y, 1, 3) + at_least(3 - y, 1, 3) + at_least(x, 1, 3) + at_least(3 - x, 1, 3)

    def planes(step):
        return at_least(z, step, 7) + at_least(7 - z, step, 7)

    def signal(sem, seq, core):
        pl.semaphore_signal(sem, inc=1, device_id=(seq, core), device_id_type=MESH)

    signal(barrier, f, o)
    for ok, seq in ((f > 0, f - 1), (f < NF - 1, f + 1)):
        @pl.when(ok)
        def _():
            signal(barrier, seq, t)
            signal(barrier, seq, o)

    near(lambda seq: signal(barrier, seq, t))
    ahead(1, lambda seq: signal(barrier, seq, t))

    loads[0].wait()
    frames[1, t] = lat[...]

    width = ea.shape[1]
    loads[1].wait()
    bias = three(eb[...].reshape(1, width))
    ea[64:80] = rows_of(bias + bias, 16, width).astype(BF16)
    ea[80:128] = jnp.zeros((48, width), BF16)

    loads[4].wait()
    loads[5].wait()
    wide = jnp.concatenate([cw[...].astype(F32), rows_of(three(cb[...]), 32, 128)], axis=0)
    cwt[...] = wide.T.astype(BF16)
    pat[864:896] = jnp.ones((32, TOK), BF16)

    pl.semaphore_wait(barrier, 1 + 2 * at_least(f, 1, NF - 1) + 2 * at_least(NF - 1 - f, 1, NF - 1) + around + planes(1))

    def halo(i):
        slot, step, core = ((1, 0, o), (0, 1, t), (0, 1, o), (2, -1, t), (2, -1, o))[i]
        return pltpu.make_async_remote_copy(
            src_ref=lat, dst_ref=frames.at[slot, t], send_sem=hs.at[i], recv_sem=hr.at[slot, t],
            device_id=((f + step + NF) % NF, core), device_id_type=MESH)

    def halos(act):
        act(halo(0))

        @pl.when(f < NF - 1)
        def _():
            act(halo(1))
            act(halo(2))

        @pl.when(f > 0)
        def _():
            act(halo(3))
            act(halo(4))

    halos(lambda copy: copy.start())
    near(lambda seq: signal(tok.at[0], seq, t))
    ahead(1, lambda seq: signal(ztok.at[0], seq, t))

    lane = lax.broadcasted_iota(jnp.int32, (HEADS * DH, 128), 1)
    low = ((lane >= 32) & (lane < 64)) | (lane >= 67)

    loads[2].wait()
    loads[3].wait()
    loads[6].wait()

    def fold(i, c):
        wcopy(i, 0).wait()
        wcopy(i, 1).wait()
        full = nt(w[i], ea[...])
        hi = full.astype(BF16).astype(F32)
        g[i] = jnp.where(low, full - hi, hi).astype(BF16)
        return c

    fold(1, 0)
    fold(2, 0)
    fold(0, 0)

    pl.semaphore_wait(tok.at[0], around)
    floor = z * PLANE
    signal(tok.at[1], floor + x * 4 + (y + 2) % 4, t)
    signal(tok.at[1], floor + (p + 8) % PLANE, t)
    def fill(i, c):
        target = lax.broadcasted_iota(jnp.int32, (128, TOK), 1)
        source = lax.broadcasted_iota(jnp.int32, (128, TOK), 0)
        hit = ((target & 7) == i) & ((target >> 3) == source)
        perm[pl.ds(pl.multiple_of(i * 128, 128), 128)] = jnp.where(hit, 1.0, 0.0).astype(BF16)
        return c

    lax.fori_loop(0, 8, fill, 0)
    sx[...] = jnp.zeros_like(sx)

    def arrived(slot, core):
        pltpu.make_async_remote_copy(
            src_ref=lat, dst_ref=frames.at[slot, core], send_sem=hs.at[0], recv_sem=hr.at[slot, core],
            device_id=(f, o), device_id_type=MESH).wait_recv()

    arrived(1, o)
    for ok, slot in ((f > 0, 0), (f < NF - 1, 2)):
        @pl.when(ok)
        def _():
            arrived(slot, t)
            arrived(slot, o)

    row = lax.broadcasted_iota(jnp.int32, (32, TOK), 1) & 127
    none = jnp.zeros((32, 128), BF16)
    here = None
    for a in range(3):
        x = jnp.concatenate([frames[a, c // 4, c % 4] for c in range(8)], axis=1).astype(F32)
        if a == 0:
            x = jnp.where(f > 0, x, 0.0)
        if a == 2:
            x = jnp.where(f < NF - 1, x, 0.0)
        if a == 1:
            here = x
        shifted = (
            jnp.where(row == 0, 0.0, pltpu.roll(x, 1, 1)),
            x,
            jnp.where(row == 127, 0.0, pltpu.roll(x, TOK - 1, 1)),
        )
        for b in range(3):
            moved = shifted[b].astype(BF16)
            at = (a * 3 + b) * 96
            pat[at : at + 32] = jnp.concatenate([none, moved[:, : TOK - 128]], axis=1)
            pat[at + 32 : at + 64] = moved
            pat[at + 64 : at + 96] = jnp.concatenate([moved[:, 128:], none], axis=1)
    pl.semaphore_wait(ztok.at[0], planes(1))
    ahead(2, lambda seq: signal(ztok.at[1], seq, t))
    pl.semaphore_wait(tok.at[1], 2)
    for k in range(1, 4):
        signal(tok.at[2], floor + (p + 4 * k) % PLANE, t)
    conv = nn(cwt[...], pat[...])
    act = (conv / (1.0 + jnp.exp(-conv))).astype(BF16)
    mixed = (nn(pw[...], act) + here).astype(BF16)
    maug[0:32] = mixed
    maug[32:64] = mixed
    maug[64:80] = jnp.ones((16, TOK), BF16)
    maug[80:128] = jnp.zeros((48, TOK), BF16)

    kt[...] = jnp.maximum(nn(g[1], maug[...]), 0.0).astype(BF16)
    plus = maug[32:80]
    for h in range(HEADS):
        s = nt(plus, kt[h * DH : (h + 1) * DH])
        sx[2 * h, :, 0:DH] = s[0:16]
        sx[2 * h + 1, :, 0:DH] = s[16:32]
        sx[10, h : h + 1, 0:DH] = s[32:33]

    pl.semaphore_wait(tok.at[2], 3)

    def along(k):
        return pltpu.make_async_remote_copy(
            src_ref=tz, dst_ref=rz.at[z], send_sem=s2.at[k], recv_sem=v2.at[z],
            device_id=((f + k * PLANE) % NF, t), device_id_type=MESH)

    def later(act):
        for k in range(1, DEPTH):
            pl.when(z + k < DEPTH)(functools.partial(act, k))

    def one(k, c):
        q = (p + k) % PLANE

        @pl.when(q < OWNERS)
        def _():
            pltpu.make_async_remote_copy(
                src_ref=sx.at[q], dst_ref=r1.at[p], send_sem=s1.at[k], recv_sem=v1.at[p],
                device_id=(z * PLANE + q, t), device_id_type=MESH).start()

        return c

    lax.fori_loop(1, PLANE, one, 0)

    pl.semaphore_wait(ztok.at[1], planes(2))
    ahead(4, lambda seq: signal(ztok.at[2], seq, t), "only")

    def queries():
        qaug[...] = nn(maug[...], perm[...]).astype(BF16)
        qt[...] = jnp.maximum(nn(g[0], qaug[...]), 0.0).astype(BF16)

    @pl.when(p < OWNERS)
    def _():
        r1[p] = sx[p]

        def got(k, c):
            q = (p + k) % PLANE
            pltpu.make_async_remote_copy(
                src_ref=sx.at[0], dst_ref=r1.at[q], send_sem=s1.at[0], recv_sem=v1.at[q],
                device_id=(f, o), device_id_type=MESH).wait_recv()
            return c

        lax.fori_loop(1, PLANE, got, 0)
        total = r1[0]
        for i in range(1, PLANE):
            total = total + r1[i]
        tz[...] = total
        pl.when(z < 4)(functools.partial(pl.semaphore_wait, ztok.at[2], 1))
        later(lambda k: along(k).start())
        run = jnp.zeros((16, 128), F32)
        for i in range(PLANE):
            p3[i] = run
            run = run + r1[i]

    @pl.when((p >= OWNERS) & (z < 4))
    def _():
        pl.semaphore_wait(ztok.at[2], 1)

    queries()

    @pl.when(p < OWNERS)
    def _():
        def got(k, c):
            @pl.when(k < z)
            def _():
                pltpu.make_async_remote_copy(
                    src_ref=tz, dst_ref=rz.at[k], send_sem=s2.at[0], recv_sem=v2.at[k],
                    device_id=(f, o), device_id_type=MESH).wait_recv()

            return c

        lax.fori_loop(0, DEPTH - 1, got, 0)
        before = jnp.zeros((16, 128), F32)
        for i in range(DEPTH - 1):
            before = before + jnp.where(i < z, rz[i], 0.0)
        for i in range(PLANE):
            p3[i] = p3[i] + before

        def three_(k, c):
            q = (p + k) % PLANE
            pltpu.make_async_remote_copy(
                src_ref=p3.at[q], dst_ref=px.at[p], send_sem=s3.at[k], recv_sem=v3.at[p],
                device_id=(z * PLANE + q, t), device_id_type=MESH).start()
            return c

        lax.fori_loop(1, PLANE, three_, 0)
        px[p] = p3[p]

    def back(k, c):
        q = (p + k) % PLANE

        @pl.when(q < OWNERS)
        def _():
            pltpu.make_async_remote_copy(
                src_ref=p3.at[0], dst_ref=px.at[q], send_sem=s3.at[0], recv_sem=v3.at[q],
                device_id=(f, o), device_id_type=MESH).wait_recv()

        return c

    lax.fori_loop(1, PLANE, back, 0)

    gv_out[...] = g[2]
    for i in range(OWNERS):
        total_out[i] = px[i] + sx[i]

    halos(lambda copy: copy.wait_send())

    def sent(k, c):
        @pl.when((p + k) % PLANE < OWNERS)
        def _():
            pltpu.make_async_remote_copy(
                src_ref=sx.at[0], dst_ref=r1.at[0], send_sem=s1.at[k], recv_sem=v1.at[0],
                device_id=(f, o), device_id_type=MESH).wait_send()

        @pl.when(p < OWNERS)
        def _():
            pltpu.make_async_remote_copy(
                src_ref=p3.at[0], dst_ref=px.at[0], send_sem=s3.at[k], recv_sem=v3.at[0],
                device_id=(f, o), device_id_type=MESH).wait_send()

        return c

    lax.fori_loop(1, PLANE, sent, 0)

    @pl.when(p < OWNERS)
    def _():
        later(lambda k: along(k).wait_send())


def finish(tot, gvs, qts, out_hbm, stage, sem):
    norms = tot[10]
    for h in range(HEADS):
        s = jnp.concatenate(
            [tot[2 * h], tot[2 * h + 1], jnp.broadcast_to(norms[h : h + 1], (16, 128))], axis=0)[:, 0:DH]
        hi = s.astype(BF16)
        lo = (s - hi.astype(F32)).astype(BF16)
        both = nn(jnp.concatenate([hi, lo], axis=0), qts[h * DH : (h + 1) * DH])
        n = both[0:48] + both[48:96]
        den = n[32:33]
        inv = 1.0 / (den + EPS)
        r = n[0:32] * jnp.broadcast_to(inv, (32, TOK))
        ratio = jnp.broadcast_to(den * inv, (16, TOK))
        parts = jnp.concatenate([r, r, ratio], axis=0)
        top = parts.astype(BF16)
        rest = (parts - top.astype(F32)).astype(BF16)
        gv = gvs[h * DH : (h + 1) * DH, 0:80]
        stage[h] = (nn(gv, top) + nn(gv, rest)).astype(BF16)
        pltpu.make_async_copy(stage.at[h], out_hbm.at[h], sem.at[h]).start()
    for h in range(HEADS):
        pltpu.make_async_copy(stage.at[h], out_hbm.at[h], sem.at[h]).wait()


def per_device(latent, conv_weight, conv_bias, proj_weight, embed_weight, embed_bias, qkv_weight):
    width = embed_weight.shape[1]
    lat = jnp.transpose(latent, (1, 3, 2, 0)).reshape(4, 32, 128)
    vmem, anywhere = pl.BlockSpec(memory_space=pltpu.VMEM), pl.BlockSpec(memory_space=pl.ANY)
    dma, vm = pltpu.SemaphoreType.DMA, pltpu.VMEM
    parts = pl.pallas_call(
        kernel,
        out_shape=[
            jax.ShapeDtypeStruct((OWNERS, 16, 128), F32),
            jax.ShapeDtypeStruct((HEADS * DH, 128), BF16),
            jax.ShapeDtypeStruct((HEADS * DH, TOK), BF16),
        ],
        in_specs=[anywhere] * 7,
        out_specs=[vmem] * 3,
        scratch_shapes=[
            vm((4, 32, 128), BF16),
            vm((864, 128), BF16),
            vm((1, 128), F32),
            vm((32, 128), BF16),
            vm((width,), F32),
            vm((3, 2, 4, 32, 128), BF16),
            vm((3, HEADS * DH, width), BF16),
            vm((128, width), BF16),
            vm((3, HEADS * DH, 128), BF16),
            vm((128, 896), BF16),
            vm((896, TOK), BF16),
            vm((128, TOK), BF16),
            vm((128, TOK), BF16),
            vm((TOK, TOK), BF16),
            vm((HEADS * DH, TOK), BF16),
            vm((OWNERS, 16, 128), F32),
            vm((PLANE, 16, 128), F32),
            vm((DEPTH, 16, 128), F32),
            vm((16, 128), F32),
            vm((PLANE, 16, 128), F32),
            vm((OWNERS, 16, 128), F32),
            dma((7,)), dma((5,)), dma((3, 2)), dma((3, 2)),
            dma((PLANE,)), dma((PLANE,)), dma((DEPTH,)), dma((DEPTH,)), dma((PLANE,)), dma((PLANE,)),
            pltpu.SemaphoreType.REGULAR((3,)), pltpu.SemaphoreType.REGULAR((3,)),
        ],
        compiler_params=pltpu.CompilerParams(collective_id=0, has_side_effects=True, vmem_limit_bytes=40 << 20),
    )(*(pltpu.with_memory_space_constraint(v, pltpu.HBM) for v in (
        lat, conv_weight.reshape(864, 128), conv_bias.reshape(1, 128), jnp.transpose(proj_weight),
        embed_weight, embed_bias, jnp.transpose(qkv_weight, (0, 2, 1)),
    )))
    out = pl.pallas_call(
        finish,
        out_shape=jax.ShapeDtypeStruct((HEADS, DH, TOK), BF16),
        in_specs=[vmem] * 3,
        out_specs=anywhere,
        scratch_shapes=[
            vm((HEADS, DH, TOK), BF16), dma((HEADS,)),
        ],
        compiler_params=pltpu.CompilerParams(vmem_limit_bytes=16 << 20),
    )(*parts)
    return jnp.transpose(out.reshape(HEADS * DH, TOK))


def solution(mesh):
    return jax.shard_map(
        per_device,
        mesh=mesh,
        in_specs=(P(None, "tp", None, "seq"), P(), P(), P(), P(), P(), P(None, None, "tp")),
        out_specs=P("seq", "tp"),
        check_vma=False,
    )
```

time: 38.7 us -> 31.3 us (0.81)
  the two profiles are of different devices: /device:TPU:1 before, /device:TPU:224 now
where the time goes in v2:
time: 31.3 us; the launch traced here: 31.2 us
  Pallas kernels  31.2 us (100%)
    pallas_call x1, Pallas kernels, per_device(): pl.pallas_call(kernel, out_shape=[jax.ShapeDtypeStruct((OWNERS, 16, 128),...  28.8 us
    pallas_call x1, Pallas kernels, per_device(): pl.pallas_call(finish, out_shape=jax.ShapeDtypeStruct((HEADS, DH, TOK), B...  2.41 us

profile of v2, /device:TPU:224, one launch (start us, length us, event | category | flops | bytes accessed | tf_op | source)
XLA Modules:
  0.0 31.2 jit_solution(5423222532327881398)
XLA Ops:
  0.0 28.8 %shard_map.73 = (f32[11,16,128]{2,1,0:T(8,128)S(1)}, bf16[560,128]{1,0:T(8,128)(2,1)S(1)}, bf16[560,1024]{1,0:T(8,128)(2,1)S(1)}) custom-call(bf16[4,32,128]{2,1,0:T(8,128)(2,1)} %bitcast.14, bf16[864,128]{1,0:T(8,128)(2,1)} %bitcast.13, f32[1,128]{1,0:T(1,128)} %bitcast.16, bf16[32,128]{1,0:T(8,128)(2,1)} %bitcast.15, bf16[32,2240]{1,0:T(8,128)(2,1)} %ew_hbm.1, ...), custom_call_target="tpu_custom_call" | custom-call | tf_op jit(solution)/shard_map/pallas_call | solution.py:393
  28.8 2.4 %shard_map.74 = bf16[5,112,1024]{2,1,0:T(8,128)(2,1)} custom-call(f32[11,16,128]{2,1,0:T(8,128)S(1)} %get-tuple-element.8.tot, bf16[560,128]{1,0:T(8,128)(2,1)S(1)} %get-tuple-element.9.gvs, bf16[560,1024]{1,0:T(8,128)(2,1)S(1)} %get-tuple-element.10.qts), custom_call_target="tpu_custom_call" | custom-call | tf_op jit(solution)/shard_map/pallas_call | solution.py:433

commit v3 on v2

--- a/solution.py
+++ b/solution.py
@@ -45,7 +45,7 @@
 
 def kernel(
     lat_hbm, cw_hbm, cb_hbm, pw_hbm, ew_hbm, eb_hbm, w_hbm, total_out, gv_out, qt,
-    lat, cw, cb, pw, eb, frames, w, ea, g, cwt, pat, maug, qaug, perm, kt, sx, r1, rz, tz, p3, px,
+    lat, cw, cb, pw, eb, frames, w, ea, g, cwt, pat, maug, qaug, perm, kt, acc, sx, r1, rz, tz, p3, px,
     ls, hs, hr, ws, s1, v1, s2, v2, s3, v3, tok, ztok,
 ):
     f = lax.axis_index("seq")
@@ -54,6 +54,39 @@
     o = 1 - t
     x, y = p // 4, p % 4
 
+    barrier = pltpu.get_barrier_semaphore()
+
+    def near(act):
+        for ok, seq in ((y > 0, f - 1), (y < 3, f + 1), (x > 0, f - 4), (x < 3, f + 4)):
+            pl.when(ok)(functools.partial(act, seq))
+
+    def ahead(step, act, back=True):
+        if back:
+            pl.when(z >= step)(functools.partial(act, f - step * PLANE))
+        if back != "only":
+            pl.when(z < DEPTH - step)(functools.partial(act, f + step * PLANE))
+
+    def at_least(value, least, top):
+        return (value + top + 1 - least) // (top + 1)
+
+    around = at_least(y, 1, 3) + at_least(3 - y, 1, 3) + at_least(x, 1, 3) + at_least(3 - x, 1, 3)
+
+    def planes(step):
+        return at_least(z, step, 7) + at_least(7 - z, step, 7)
+
+    def signal(sem, seq, core):
+        pl.semaphore_signal(sem, inc=1, device_id=(seq, core), device_id_type=MESH)
+
+    signal(barrier, f, o)
+    for ok, seq in ((f > 0, f - 1), (f < NF - 1, f + 1)):
+        @pl.when(ok)
+        def _():
+            signal(barrier, seq, t)
+            signal(barrier, seq, o)
+
+    near(lambda seq: signal(barrier, seq, t))
+    ahead(1, lambda seq: signal(barrier, seq, t))
+
     def load(src, dst, i):
         return pltpu.make_async_copy(src, dst, ls.at[i])
 
@@ -71,39 +104,6 @@
     for i in (1, 2, 0):
         for half in range(2):
             wcopy(i, half).start()
-
-    barrier = pltpu.get_barrier_semaphore()
-
-    def near(act):
-        for ok, seq in ((y > 0, f - 1), (y < 3, f + 1), (x > 0, f - 4), (x < 3, f + 4)):
-            pl.when(ok)(functools.partial(act, seq))
-
-    def ahead(step, act, back=True):
-        if back:
-            pl.when(z >= step)(functools.partial(act, f - step * PLANE))
-        if back != "only":
-            pl.when(z < DEPTH - step)(functools.partial(act, f + step * PLANE))
-
-    def at_least(value, least, top):
-        return (value + top + 1 - least) // (top + 1)
-
-    around = at_least(y, 1, 3) + at_least(3 - y, 1, 3) + at_least(x, 1, 3) + at_least(3 - x, 1, 3)
-
-    def planes(step):
-        return at_least(z, step, 7) + at_least(7 - z, step, 7)
-
-    def signal(sem, seq, core):
-        pl.semaphore_signal(sem, inc=1, device_id=(seq, core), device_id_type=MESH)
-
-    signal(barrier, f, o)
-    for ok, seq in ((f > 0, f - 1), (f < NF - 1, f + 1)):
-        @pl.when(ok)
-        def _():
-            signal(barrier, seq, t)
-            signal(barrier, seq, o)
-
-    near(lambda seq: signal(barrier, seq, t))
-    ahead(1, lambda seq: signal(barrier, seq, t))
 
     loads[0].wait()
     frames[1, t] = lat[...]
@@ -161,13 +161,12 @@
         return c
 
     fold(1, 0)
-    fold(2, 0)
-    fold(0, 0)
 
     pl.semaphore_wait(tok.at[0], around)
     floor = z * PLANE
     signal(tok.at[1], floor + x * 4 + (y + 2) % 4, t)
     signal(tok.at[1], floor + (p + 8) % PLANE, t)
+
     def fill(i, c):
         target = lax.broadcasted_iota(jnp.int32, (128, TOK), 1)
         source = lax.broadcasted_iota(jnp.int32, (128, TOK), 0)
@@ -183,28 +182,17 @@
             src_ref=lat, dst_ref=frames.at[slot, core], send_sem=hs.at[0], recv_sem=hr.at[slot, core],
             device_id=(f, o), device_id_type=MESH).wait_recv()
 
-    arrived(1, o)
-    for ok, slot in ((f > 0, 0), (f < NF - 1, 2)):
-        @pl.when(ok)
-        def _():
-            arrived(slot, t)
-            arrived(slot, o)
-
     row = lax.broadcasted_iota(jnp.int32, (32, TOK), 1) & 127
     none = jnp.zeros((32, 128), BF16)
-    here = None
-    for a in range(3):
-        x = jnp.concatenate([frames[a, c // 4, c % 4] for c in range(8)], axis=1).astype(F32)
-        if a == 0:
-            x = jnp.where(f > 0, x, 0.0)
-        if a == 2:
-            x = jnp.where(f < NF - 1, x, 0.0)
-        if a == 1:
-            here = x
+
+    def frame(a):
+        return jnp.concatenate([frames[a, c // 4, c % 4] for c in range(8)], axis=1).astype(F32)
+
+    def patches(a, image):
         shifted = (
-            jnp.where(row == 0, 0.0, pltpu.roll(x, 1, 1)),
-            x,
-            jnp.where(row == 127, 0.0, pltpu.roll(x, TOK - 1, 1)),
+            jnp.where(row == 0, 0.0, pltpu.roll(image, 1, 1)),
+            image,
+            jnp.where(row == 127, 0.0, pltpu.roll(image, TOK - 1, 1)),
         )
         for b in range(3):
             moved = shifted[b].astype(BF16)
@@ -212,12 +200,32 @@
             pat[at : at + 32] = jnp.concatenate([none, moved[:, : TOK - 128]], axis=1)
             pat[at + 32 : at + 64] = moved
             pat[at + 64 : at + 96] = jnp.concatenate([moved[:, 128:], none], axis=1)
+
+    arrived(1, o)
+    here = frame(1)
+    patches(1, here)
+
+    @pl.when(f > 0)
+    def _():
+        arrived(0, t)
+        arrived(0, o)
+
+    patches(0, jnp.where(f > 0, frame(0), 0.0))
+    acc[...] = nn(cwt[:, 0:576], pat[0:576])
+
     pl.semaphore_wait(ztok.at[0], planes(1))
     ahead(2, lambda seq: signal(ztok.at[1], seq, t))
     pl.semaphore_wait(tok.at[1], 2)
     for k in range(1, 4):
         signal(tok.at[2], floor + (p + 4 * k) % PLANE, t)
-    conv = nn(cwt[...], pat[...])
+
+    @pl.when(f < NF - 1)
+    def _():
+        arrived(2, t)
+        arrived(2, o)
+
+    patches(2, jnp.where(f < NF - 1, frame(2), 0.0))
+    conv = acc[...] + nn(cwt[:, 576:896], pat[576:896])
     act = (conv / (1.0 + jnp.exp(-conv))).astype(BF16)
     mixed = (nn(pw[...], act) + here).astype(BF16)
     maug[0:32] = mixed
@@ -241,26 +249,29 @@
             device_id=((f + k * PLANE) % NF, t), device_id_type=MESH)
 
     def later(act):
-        for k in range(1, DEPTH):
+        for k in (4, 3, 5, 2, 6, 1, 7):
             pl.when(z + k < DEPTH)(functools.partial(act, k))
 
-    def one(k, c):
-        q = (p + k) % PLANE
-
+    peers = sorted(((a, b) for a in range(4) for b in range(4) if a or b), key=lambda c: -sum(min(v, 4 - v) for v in c))
+
+    def across(act):
+        for k, (a, b) in enumerate(peers):
+            act(k, (x + a) % 4 * 4 + (y + b) % 4)
+
+    def one(k, q):
         @pl.when(q < OWNERS)
         def _():
             pltpu.make_async_remote_copy(
                 src_ref=sx.at[q], dst_ref=r1.at[p], send_sem=s1.at[k], recv_sem=v1.at[p],
-                device_id=(z * PLANE + q, t), device_id_type=MESH).start()
-
-        return c
-
-    lax.fori_loop(1, PLANE, one, 0)
+                device_id=(floor + q, t), device_id_type=MESH).start()
+
+    across(one)
 
     pl.semaphore_wait(ztok.at[1], planes(2))
     ahead(4, lambda seq: signal(ztok.at[2], seq, t), "only")
 
     def queries():
+        fold(0, 0)
         qaug[...] = nn(maug[...], perm[...]).astype(BF16)
         qt[...] = jnp.maximum(nn(g[0], qaug[...]), 0.0).astype(BF16)
 
@@ -311,15 +322,16 @@
         for i in range(PLANE):
             p3[i] = p3[i] + before
 
-        def three_(k, c):
-            q = (p + k) % PLANE
+        def three_(k, q):
             pltpu.make_async_remote_copy(
                 src_ref=p3.at[q], dst_ref=px.at[p], send_sem=s3.at[k], recv_sem=v3.at[p],
-                device_id=(z * PLANE + q, t), device_id_type=MESH).start()
-            return c
-
-        lax.fori_loop(1, PLANE, three_, 0)
+                device_id=(floor + q, t), device_id_type=MESH).start()
+
+        across(three_)
         px[p] = p3[p]
+
+    fold(2, 0)
+    gv_out[...] = g[2]
 
     def back(k, c):
         q = (p + k) % PLANE
@@ -334,14 +346,13 @@
 
     lax.fori_loop(1, PLANE, back, 0)
 
-    gv_out[...] = g[2]
     for i in range(OWNERS):
         total_out[i] = px[i] + sx[i]
 
     halos(lambda copy: copy.wait_send())
 
-    def sent(k, c):
-        @pl.when((p + k) % PLANE < OWNERS)
+    def sent(k, q):
+        @pl.when(q < OWNERS)
         def _():
             pltpu.make_async_remote_copy(
                 src_ref=sx.at[0], dst_ref=r1.at[0], send_sem=s1.at[k], recv_sem=v1.at[0],
@@ -353,9 +364,7 @@
                 src_ref=p3.at[0], dst_ref=px.at[0], send_sem=s3.at[k], recv_sem=v3.at[0],
                 device_id=(f, o), device_id_type=MESH).wait_send()
 
-        return c
-
-    lax.fori_loop(1, PLANE, sent, 0)
+    across(sent)
 
     @pl.when(p < OWNERS)
     def _():
@@ -415,6 +424,7 @@
             vm((128, TOK), BF16),
             vm((TOK, TOK), BF16),
             vm((HEADS * DH, TOK), BF16),
+            vm((128, TOK), F32),
             vm((OWNERS, 16, 128), F32),
             vm((PLANE, 16, 128), F32),
             vm((DEPTH, 16, 128), F32),

time: 31.3 us -> 29.2 us (0.933)
  Pallas kernels: 31.2 us -> 29.1 us
    pallas_call x1, Pallas kernels: 28.8 us -> 26.7 us  [per_device(): pl.pallas_call(kernel, out_shape=[jax.ShapeDtypeStruct((OWNERS, 16, 128),...]
where the time goes in v3:
time: 29.2 us; the launch traced here: 29.1 us
  Pallas kernels  29.1 us (100%)
    pallas_call x1, Pallas kernels, per_device(): pl.pallas_call(kernel, out_shape=[jax.ShapeDtypeStruct((OWNERS, 16, 128),...  26.7 us
    pallas_call x1, Pallas kernels, per_device(): pl.pallas_call(finish, out_shape=jax.ShapeDtypeStruct((HEADS, DH, TOK), B...  2.4 us

profile of v3, /device:TPU:224, one launch (start us, length us, event | category | flops | bytes accessed | tf_op | source)
XLA Modules:
  0.0 29.1 jit_solution(90293206098618848)
XLA Ops:
  0.0 26.7 %shard_map.73 = (f32[11,16,128]{2,1,0:T(8,128)S(1)}, bf16[560,128]{1,0:T(8,128)(2,1)S(1)}, bf16[560,1024]{1,0:T(8,128)(2,1)S(1)}) custom-call(bf16[4,32,128]{2,1,0:T(8,128)(2,1)} %bitcast.14, bf16[864,128]{1,0:T(8,128)(2,1)} %bitcast.13, f32[1,128]{1,0:T(1,128)} %bitcast.16, bf16[32,128]{1,0:T(8,128)(2,1)} %bitcast.15, bf16[32,2240]{1,0:T(8,128)(2,1)} %ew_hbm.1, ...), custom_call_target="tpu_custom_call" | custom-call | tf_op jit(solution)/shard_map/pallas_call | solution.py:402
  26.7 2.4 %shard_map.74 = bf16[5,112,1024]{2,1,0:T(8,128)(2,1)} custom-call(f32[11,16,128]{2,1,0:T(8,128)S(1)} %get-tuple-element.8.tot, bf16[560,128]{1,0:T(8,128)(2,1)S(1)} %get-tuple-element.9.gvs, bf16[560,1024]{1,0:T(8,128)(2,1)S(1)} %get-tuple-element.10.qts), custom_call_target="tpu_custom_call" | custom-call | tf_op jit(solution)/shard_map/pallas_call | solution.py:443

commit v4 on v3

--- a/solution.py
+++ b/solution.py
@@ -69,6 +69,12 @@
     def at_least(value, least, top):
         return (value + top + 1 - least) // (top + 1)
 
+    def owns(q):
+        return (q != 5) & (q != 6) & (q != 9) & (q != 10) & (q != 15)
+
+    def slice_of(q):
+        return q - at_least(q, 6, 15) - at_least(q, 7, 15) - at_least(q, 10, 15) - at_least(q, 11, 15)
+
     around = at_least(y, 1, 3) + at_least(3 - y, 1, 3) + at_least(x, 1, 3) + at_least(3 - x, 1, 3)
 
     def planes(step):
@@ -108,6 +114,31 @@
     loads[0].wait()
     frames[1, t] = lat[...]
 
+    pl.semaphore_wait(barrier, 1 + 2 * at_least(f, 1, NF - 1) + 2 * at_least(NF - 1 - f, 1, NF - 1) + around + planes(1))
+
+    def halo(i):
+        slot, step, core = ((1, 0, o), (0, 1, t), (0, 1, o), (2, -1, t), (2, -1, o))[i]
+        return pltpu.make_async_remote_copy(
+            src_ref=lat, dst_ref=frames.at[slot, t], send_sem=hs.at[i], recv_sem=hr.at[slot, t],
+            device_id=((f + step + NF) % NF, core), device_id_type=MESH)
+
+    def halos(act):
+        @pl.when(f < NF - 1)
+        def _():
+            act(halo(1))
+            act(halo(2))
+
+        @pl.when(f > 0)
+        def _():
+            act(halo(3))
+            act(halo(4))
+
+        act(halo(0))
+
+    halos(lambda copy: copy.start())
+    near(lambda seq: signal(tok.at[0], seq, t))
+    ahead(1, lambda seq: signal(ztok.at[0], seq, t))
+
     width = ea.shape[1]
     loads[1].wait()
     bias = three(eb[...].reshape(1, width))
@@ -116,34 +147,11 @@
 
     loads[4].wait()
     loads[5].wait()
-    wide = jnp.concatenate([cw[...].astype(F32), rows_of(three(cb[...]), 32, 128)], axis=0)
-    cwt[...] = wide.T.astype(BF16)
-    pat[864:896] = jnp.ones((32, TOK), BF16)
-
-    pl.semaphore_wait(barrier, 1 + 2 * at_least(f, 1, NF - 1) + 2 * at_least(NF - 1 - f, 1, NF - 1) + around + planes(1))
-
-    def halo(i):
-        slot, step, core = ((1, 0, o), (0, 1, t), (0, 1, o), (2, -1, t), (2, -1, o))[i]
-        return pltpu.make_async_remote_copy(
-            src_ref=lat, dst_ref=frames.at[slot, t], send_sem=hs.at[i], recv_sem=hr.at[slot, t],
-            device_id=((f + step + NF) % NF, core), device_id_type=MESH)
-
-    def halos(act):
-        act(halo(0))
-
-        @pl.when(f < NF - 1)
-        def _():
-            act(halo(1))
-            act(halo(2))
-
-        @pl.when(f > 0)
-        def _():
-            act(halo(3))
-            act(halo(4))
-
-    halos(lambda copy: copy.start())
-    near(lambda seq: signal(tok.at[0], seq, t))
-    ahead(1, lambda seq: signal(ztok.at[0], seq, t))
+    bias_rows = rows_of(three(cb[...]), 32, 128)
+    for a in range(3):
+        wide = [cw[a * 288 : a * 288 + 288].astype(F32), bias_rows if a == 1 else jnp.zeros((32, 128), F32)]
+        cwt[a] = jnp.concatenate(wide, axis=0).T.astype(BF16)
+        pat[a, 288:320] = jnp.ones((32, TOK), BF16)
 
     lane = lax.broadcasted_iota(jnp.int32, (HEADS * DH, 128), 1)
     low = ((lane >= 32) & (lane < 64)) | (lane >= 67)
@@ -196,22 +204,14 @@
         )
         for b in range(3):
             moved = shifted[b].astype(BF16)
-            at = (a * 3 + b) * 96
-            pat[at : at + 32] = jnp.concatenate([none, moved[:, : TOK - 128]], axis=1)
-            pat[at + 32 : at + 64] = moved
-            pat[at + 64 : at + 96] = jnp.concatenate([moved[:, 128:], none], axis=1)
+            at = b * 96
+            pat[a, at : at + 32] = jnp.concatenate([none, moved[:, : TOK - 128]], axis=1)
+            pat[a, at + 32 : at + 64] = moved
+            pat[a, at + 64 : at + 96] = jnp.concatenate([moved[:, 128:], none], axis=1)
 
     arrived(1, o)
     here = frame(1)
     patches(1, here)
-
-    @pl.when(f > 0)
-    def _():
-        arrived(0, t)
-        arrived(0, o)
-
-    patches(0, jnp.where(f > 0, frame(0), 0.0))
-    acc[...] = nn(cwt[:, 0:576], pat[0:576])
 
     pl.semaphore_wait(ztok.at[0], planes(1))
     ahead(2, lambda seq: signal(ztok.at[1], seq, t))
@@ -219,13 +219,30 @@
     for k in range(1, 4):
         signal(tok.at[2], floor + (p + 4 * k) % PLANE, t)
 
-    @pl.when(f < NF - 1)
-    def _():
-        arrived(2, t)
-        arrived(2, o)
-
-    patches(2, jnp.where(f < NF - 1, frame(2), 0.0))
-    conv = acc[...] + nn(cwt[:, 576:896], pat[576:896])
+    last = jnp.where(y == 0, 0, 2)
+
+    def frame_of(a):
+        columns = [frames[a, c // 4, c % 4] for c in range(8)]
+        image = jnp.concatenate(columns, axis=1).astype(F32)
+        return jnp.where(f + a - 1 < 0, 0.0, jnp.where(f + a - 1 > NF - 1, 0.0, image))
+
+    def come(a):
+        @pl.when((f + a - 1 >= 0) & (f + a - 1 < NF))
+        def _():
+            arrived(a, t)
+            arrived(a, o)
+
+    come(2 - last)
+    patches(2 - last, frame_of(2 - last))
+    acc[...] = nn(cwt[1], pat[1]) + nn(cwt[2 - last], pat[2 - last])
+    come(last)
+    patches(last, frame_of(last))
+    @pl.when(z >= 4)
+    def _():
+        pl.semaphore_wait(ztok.at[1], planes(2))
+        signal(ztok.at[2], f - 4 * PLANE, t)
+
+    conv = acc[...] + nn(cwt[last], pat[last])
     act = (conv / (1.0 + jnp.exp(-conv))).astype(BF16)
     mixed = (nn(pw[...], act) + here).astype(BF16)
     maug[0:32] = mixed
@@ -248,8 +265,8 @@
             src_ref=tz, dst_ref=rz.at[z], send_sem=s2.at[k], recv_sem=v2.at[z],
             device_id=((f + k * PLANE) % NF, t), device_id_type=MESH)
 
-    def later(act):
-        for k in (4, 3, 5, 2, 6, 1, 7):
+    def later(act, steps=range(1, DEPTH)):
+        for k in steps:
             pl.when(z + k < DEPTH)(functools.partial(act, k))
 
     peers = sorted(((a, b) for a in range(4) for b in range(4) if a or b), key=lambda c: -sum(min(v, 4 - v) for v in c))
@@ -259,25 +276,27 @@
             act(k, (x + a) % 4 * 4 + (y + b) % 4)
 
     def one(k, q):
-        @pl.when(q < OWNERS)
-        def _():
-            pltpu.make_async_remote_copy(
-                src_ref=sx.at[q], dst_ref=r1.at[p], send_sem=s1.at[k], recv_sem=v1.at[p],
+        @pl.when(owns(q))
+        def _():
+            pltpu.make_async_remote_copy(
+                src_ref=sx.at[slice_of(q)], dst_ref=r1.at[p], send_sem=s1.at[k], recv_sem=v1.at[p],
                 device_id=(floor + q, t), device_id_type=MESH).start()
 
     across(one)
 
-    pl.semaphore_wait(ztok.at[1], planes(2))
-    ahead(4, lambda seq: signal(ztok.at[2], seq, t), "only")
+    @pl.when(z < 4)
+    def _():
+        pl.semaphore_wait(ztok.at[1], planes(2))
+
 
     def queries():
         fold(0, 0)
         qaug[...] = nn(maug[...], perm[...]).astype(BF16)
         qt[...] = jnp.maximum(nn(g[0], qaug[...]), 0.0).astype(BF16)
 
-    @pl.when(p < OWNERS)
-    def _():
-        r1[p] = sx[p]
+    @pl.when(owns(p))
+    def _():
+        r1[p] = sx[slice_of(p)]
 
         def got(k, c):
             q = (p + k) % PLANE
@@ -291,20 +310,19 @@
         for i in range(1, PLANE):
             total = total + r1[i]
         tz[...] = total
+        later(lambda k: along(k).start(), (4, 3, 2, 1))
         pl.when(z < 4)(functools.partial(pl.semaphore_wait, ztok.at[2], 1))
-        later(lambda k: along(k).start())
+        later(lambda k: along(k).start(), (5, 6, 7))
         run = jnp.zeros((16, 128), F32)
         for i in range(PLANE):
             p3[i] = run
             run = run + r1[i]
 
-    @pl.when((p >= OWNERS) & (z < 4))
+    @pl.when(jnp.logical_not(owns(p)) & (z < 4))
     def _():
         pl.semaphore_wait(ztok.at[2], 1)
 
-    queries()
-
-    @pl.when(p < OWNERS)
+    @pl.when(owns(p))
     def _():
         def got(k, c):
             @pl.when(k < z)
@@ -324,27 +342,24 @@
 
         def three_(k, q):
             pltpu.make_async_remote_copy(
-                src_ref=p3.at[q], dst_ref=px.at[p], send_sem=s3.at[k], recv_sem=v3.at[p],
+                src_ref=p3.at[q], dst_ref=px.at[slice_of(p)], send_sem=s3.at[k], recv_sem=v3.at[slice_of(p)],
                 device_id=(floor + q, t), device_id_type=MESH).start()
 
         across(three_)
-        px[p] = p3[p]
+        px[slice_of(p)] = p3[p]
 
     fold(2, 0)
     gv_out[...] = g[2]
-
-    def back(k, c):
-        q = (p + k) % PLANE
-
-        @pl.when(q < OWNERS)
-        def _():
-            pltpu.make_async_remote_copy(
-                src_ref=p3.at[0], dst_ref=px.at[q], send_sem=s3.at[0], recv_sem=v3.at[q],
+    queries()
+
+    def back(k, q):
+        @pl.when(owns(q))
+        def _():
+            pltpu.make_async_remote_copy(
+                src_ref=p3.at[0], dst_ref=px.at[slice_of(q)], send_sem=s3.at[0], recv_sem=v3.at[slice_of(q)],
                 device_id=(f, o), device_id_type=MESH).wait_recv()
 
-        return c
-
-    lax.fori_loop(1, PLANE, back, 0)
+    across(back)
 
     for i in range(OWNERS):
         total_out[i] = px[i] + sx[i]
@@ -352,13 +367,13 @@
     halos(lambda copy: copy.wait_send())
 
     def sent(k, q):
-        @pl.when(q < OWNERS)
+        @pl.when(owns(q))
         def _():
             pltpu.make_async_remote_copy(
                 src_ref=sx.at[0], dst_ref=r1.at[0], send_sem=s1.at[k], recv_sem=v1.at[0],
                 device_id=(f, o), device_id_type=MESH).wait_send()
 
-        @pl.when(p < OWNERS)
+        @pl.when(owns(p))
         def _():
             pltpu.make_async_remote_copy(
                 src_ref=p3.at[0], dst_ref=px.at[0], send_sem=s3.at[k], recv_sem=v3.at[0],
@@ -366,7 +381,7 @@
 
     across(sent)
 
-    @pl.when(p < OWNERS)
+    @pl.when(owns(p))
     def _():
         later(lambda k: along(k).wait_send())
 
@@ -384,11 +399,11 @@
         inv = 1.0 / (den + EPS)
         r = n[0:32] * jnp.broadcast_to(inv, (32, TOK))
         ratio = jnp.broadcast_to(den * inv, (16, TOK))
-        parts = jnp.concatenate([r, r, ratio], axis=0)
+        parts = jnp.concatenate([r, r, ratio, r, ratio], axis=0)
         top = parts.astype(BF16)
         rest = (parts - top.astype(F32)).astype(BF16)
-        gv = gvs[h * DH : (h + 1) * DH, 0:80]
-        stage[h] = (nn(gv, top) + nn(gv, rest)).astype(BF16)
+        gv = gvs[h * DH : (h + 1) * DH]
+        stage[h] = nn(jnp.concatenate([gv, gv], axis=1), jnp.concatenate([top, rest], axis=0)).astype(BF16)
         pltpu.make_async_copy(stage.at[h], out_hbm.at[h], sem.at[h]).start()
     for h in range(HEADS):
         pltpu.make_async_copy(stage.at[h], out_hbm.at[h], sem.at[h]).wait()
@@ -418,8 +433,8 @@
             vm((3, HEADS * DH, width), BF16),
             vm((128, width), BF16),
             vm((3, HEADS * DH, 128), BF16),
-            vm((128, 896), BF16),
-            vm((896, TOK), BF16),
+            vm((3, 128, 320), BF16),
+            vm((3, 320, TOK), BF16),
             vm((128, TOK), BF16),
             vm((128, TOK), BF16),
             vm((TOK, TOK), BF16),

time: 29.2 us -> 28.4 us (0.973)
  Pallas kernels: 29.1 us -> 28.3 us
    pallas_call x1, Pallas kernels: 26.7 us -> 26.1 us  [per_device(): pl.pallas_call(kernel, out_shape=[jax.ShapeDtypeStruct((OWNERS, 16, 128),...]
where the time goes in v4:
time: 28.4 us; the launch traced here: 28.3 us
  Pallas kernels  28.3 us (100%)
    pallas_call x1, Pallas kernels, per_device(): pl.pallas_call(kernel, out_shape=[jax.ShapeDtypeStruct((OWNERS, 16, 128),...  26.1 us
    pallas_call x1, Pallas kernels, per_device(): pl.pallas_call(finish, out_shape=jax.ShapeDtypeStruct((HEADS, DH, TOK), B...  2.24 us

profile of v4, /device:TPU:224, one launch (start us, length us, event | category | flops | bytes accessed | tf_op | source)
XLA Modules:
  0.0 28.3 jit_solution(6333601341557647039)
XLA Ops:
  0.0 26.1 %shard_map.73 = (f32[11,16,128]{2,1,0:T(8,128)S(1)}, bf16[560,128]{1,0:T(8,128)(2,1)S(1)}, bf16[560,1024]{1,0:T(8,128)(2,1)S(1)}) custom-call(bf16[4,32,128]{2,1,0:T(8,128)(2,1)} %bitcast.14, bf16[864,128]{1,0:T(8,128)(2,1)} %bitcast.13, f32[1,128]{1,0:T(1,128)} %bitcast.16, bf16[32,128]{1,0:T(8,128)(2,1)} %bitcast.15, bf16[32,2240]{1,0:T(8,128)(2,1)} %ew_hbm.1, ...), custom_call_target="tpu_custom_call" | custom-call | tf_op jit(solution)/shard_map/pallas_call | solution.py:417
  26.1 2.2 %shard_map.74 = bf16[5,112,1024]{2,1,0:T(8,128)(2,1)} custom-call(f32[11,16,128]{2,1,0:T(8,128)S(1)} %get-tuple-element.8.tot, bf16[560,128]{1,0:T(8,128)(2,1)S(1)} %get-tuple-element.9.gvs, bf16[560,1024]{1,0:T(8,128)(2,1)S(1)} %get-tuple-element.10.qts), custom_call_target="tpu_custom_call" | custom-call | tf_op jit(solution)/shard_map/pallas_call | solution.py:458
